TPU v7x, 32 devices: a whole 2x2x4 slice. The times are simulated.
32 devices in a mesh: dp: 16 (over z, y, x), mp: 2 (over core).
Axes of the slice: x: 2, y: 2, z: 4, core: 2. Of those that a mesh axis runs over, the one named last changes fastest.
Arguments:
- inputs: bfloat16 [32, 512, 768], P('dp'), may hold values from -6 to 6
- counts: int32 [32], P('dp'), may hold values from 16 to 128, as said below
- w_qkv: bfloat16 [768, 3, 768], P(None, None, 'mp'), may hold values from -0.21875 to 0.21875
- w_out: bfloat16 [768, 768], P('mp'), may hold values from -2 to 2
- w_up: bfloat16 [768, 3072], P(None, 'mp'), may hold values from -0.21875 to 0.21875
- w_down: bfloat16 [3072, 768], P('mp'), may hold values from -0.109375 to 0.109375
- gain_one: float32 [768], replicated, may hold values from 0.1 to 1.9
- shift_one: float32 [768], replicated, may hold values from -3 to 3
- gain_two: float32 [768], replicated, may hold values from 0.1 to 1.9
- shift_two: float32 [768], replicated, may hold values from -3 to 3
- cotangent: bfloat16 [32, 512, 768], P('dp'), may hold values from -6 to 6
Outputs:
- outputs: bfloat16 [32, 512, 768], P('dp')
- grad_inputs: float32 [32, 512, 768], P('dp')
- grad_w_qkv: float32 [768, 3, 768], P('dp', None, 'mp')
- grad_w_out: float32 [768, 768], P('mp', 'dp')
- grad_w_up: float32 [768, 3072], P('dp', 'mp')
- grad_w_down: float32 [3072, 768], P('mp', 'dp')
- grad_gain_one: float32 [768], P('dp')
- grad_shift_one: float32 [768], P('dp')
- grad_gain_two: float32 [768], P('dp')
- grad_shift_two: float32 [768], P('dp')
Inputs may be any that keep to these rules, and one draw needn't show every extreme that they name: counts[t] is the number of live query rows of table t; some table has exactly 128.
All inputs are finite; a program needn't handle non-finite values.
Results may differ from a plain program's by a relative error of at most 0.015.
The roundings to bfloat16 on the way count: a program that leaves them out, or rounds other values in their place, can miss the bound.
Values may be sent and summed in bfloat16 or wider, within the bound.
A program may use at most 128 MiB of HBM per device.

v0:
```python
from functools import partial
import math
import jax
import jax.numpy as jnp
from jax import lax
from jax.sharding import PartitionSpec as P

HD = 64
CTX = 384
EPSILON = 1e-05


def layer_norm(row_data, norm_gain, norm_shift):
    centre = jnp.mean(row_data, axis=-1, keepdims=True)
    centred = row_data - centre
    inverse = lax.rsqrt(jnp.mean(centred * centred, axis=-1, keepdims=True) + EPSILON)
    unit_rows = centred * inverse
    return (unit_rows, inverse, unit_rows * norm_gain + norm_shift)


def norm_backward(grad_norm, unit_rows, inverse, norm_gain):
    grad_unit = grad_norm * norm_gain
    grad_mean = jnp.mean(grad_unit, axis=-1, keepdims=True)
    cross_mean = jnp.mean(grad_unit * unit_rows, axis=-1, keepdims=True)
    return inverse * (grad_unit - grad_mean - unit_rows * cross_mean)


def attend_forward(query_all, key_rows, value_rows, block_rows, score_scale):
    seq_len, heads_dev, head_dim = query_all.shape
    blocks = query_all.reshape(seq_len // block_rows, block_rows, heads_dev, head_dim)

    def one_block(query_block):
        scores = (
            jnp.einsum("bhd,khd->hbk", query_block, key_rows, preferred_element_type=jnp.float32)
            * score_scale
        )
        row_peak = jnp.max(scores, axis=-1, keepdims=True)
        exp_scores = jnp.exp(scores - row_peak)
        row_total = jnp.sum(exp_scores, axis=-1, keepdims=True)
        weights = (exp_scores / row_total).astype(jnp.bfloat16)
        block_out = jnp.einsum(
            "hbk,khd->bhd", weights, value_rows, preferred_element_type=jnp.float32
        )
        return (block_out.astype(jnp.bfloat16), row_peak + jnp.log(row_total))

    heads_out, log_total = lax.map(one_block, blocks)
    return (heads_out.reshape(seq_len, heads_dev * head_dim), log_total)


def attend_backward(
    query_all, key_rows, value_rows, grad_heads, log_total, block_rows, score_scale
):
    seq_len, heads_dev, head_dim = query_all.shape
    count_blocks = seq_len // block_rows
    query_blocks = query_all.reshape(count_blocks, block_rows, heads_dev, head_dim)
    grad_blocks = grad_heads.reshape(count_blocks, block_rows, heads_dev, head_dim)

    def one_block(running, block_items):
        query_block, grad_block, lse_block = block_items
        scores = (
            jnp.einsum("bhd,khd->hbk", query_block, key_rows, preferred_element_type=jnp.float32)
            * score_scale
        )
        softmax_rows = jnp.exp(scores - lse_block)
        grad_weights = jnp.einsum(
            "bhd,khd->hbk", grad_block, value_rows, preferred_element_type=jnp.float32
        )
        row_inner = jnp.sum(softmax_rows * grad_weights, axis=-1, keepdims=True)
        grad_scores = (softmax_rows * (grad_weights - row_inner)).astype(jnp.bfloat16)
        grad_query = (
            jnp.einsum("hbk,khd->bhd", grad_scores, key_rows, preferred_element_type=jnp.float32)
            * score_scale
        ).astype(jnp.bfloat16)
        grad_key = (
            running[0]
            + jnp.einsum(
                "hbk,bhd->khd", grad_scores, query_block, preferred_element_type=jnp.float32
            )
            * score_scale
        )
        grad_value = running[1] + jnp.einsum(
            "hbk,bhd->khd",
            softmax_rows.astype(jnp.bfloat16),
            grad_block,
            preferred_element_type=jnp.float32,
        )
        return ((grad_key, grad_value), grad_query)

    empty_grad = jnp.zeros(key_rows.shape, jnp.float32)
    (grad_key, grad_value), grad_query = lax.scan(
        one_block, (empty_grad, empty_grad), (query_blocks, grad_blocks, log_total)
    )
    return (
        grad_query.reshape(seq_len, heads_dev * head_dim),
        grad_key.astype(jnp.bfloat16),
        grad_value.astype(jnp.bfloat16),
    )


def reduce_total(grads):
    return (
        lax.psum_scatter(grads[0], "dp", scatter_dimension=0, tiled=True),
        lax.psum_scatter(grads[1], "dp", scatter_dimension=1, tiled=True),
        lax.psum_scatter(grads[2], "dp", scatter_dimension=0, tiled=True),
        lax.psum_scatter(grads[3], "dp", scatter_dimension=1, tiled=True),
        lax.psum_scatter(grads[4], "dp", scatter_dimension=0, tiled=True),
        lax.psum_scatter(grads[5], "dp", scatter_dimension=0, tiled=True),
        lax.psum_scatter(grads[6], "dp", scatter_dimension=0, tiled=True),
        lax.psum_scatter(grads[7], "dp", scatter_dimension=0, tiled=True),
    )


def per_device(
    inputs, counts, w_qkv, w_out, w_up, w_down, gain_one, shift_one, gain_two, shift_two, cotangent
):
    table_count, seq_len, width = inputs.shape
    heads_dev = w_out.shape[0] // HD
    block_rows = min(512, seq_len)
    score_scale = 1.0 / math.sqrt(HD)
    positions = jnp.arange(seq_len, dtype=jnp.int32)
    results = []
    grad_list = []
    totals = None
    for table_index in range(table_count):
        row_data = inputs[table_index].astype(jnp.float32)
        live_rows = (positions < CTX + counts[table_index]).astype(jnp.float32)[:, None]
        unit_one, inverse_one, normed = layer_norm(row_data, gain_one, shift_one)
        normed = normed.astype(jnp.bfloat16)
        context = normed[:CTX]
        query_all = (
            jnp.dot(normed, w_qkv[:, 0], preferred_element_type=jnp.float32)
            .astype(jnp.bfloat16)
            .reshape(seq_len, heads_dev, HD)
        )
        key_value = jnp.einsum(
            "sd,dcn->csn", context, w_qkv[:, 1:], preferred_element_type=jnp.float32
        ).astype(jnp.bfloat16)
        key_rows = key_value[0].reshape(CTX, heads_dev, HD)
        value_rows = key_value[1].reshape(CTX, heads_dev, HD)
        heads_out, log_total = attend_forward(
            query_all, key_rows, value_rows, block_rows, score_scale
        )
        attended = lax.psum(
            jnp.dot(heads_out, w_out, preferred_element_type=jnp.float32).astype(jnp.bfloat16), "mp"
        ).astype(jnp.float32)
        resid = row_data + attended
        unit_two, inverse_two, normed_two = layer_norm(resid, gain_two, shift_two)
        normed_two = normed_two.astype(jnp.bfloat16)
        lifted = jnp.dot(normed_two, w_up, preferred_element_type=jnp.float32)
        active_full, gelu_back = jax.vjp(partial(jax.nn.gelu, approximate=False), lifted)
        active = active_full.astype(jnp.bfloat16)
        mlp_out = lax.psum(
            jnp.dot(active, w_down, preferred_element_type=jnp.float32).astype(jnp.bfloat16), "mp"
        ).astype(jnp.float32)
        results.append(((resid + mlp_out) * live_rows).astype(jnp.bfloat16))
        grad_out = cotangent[table_index].astype(jnp.float32) * live_rows
        grad_low = grad_out.astype(jnp.bfloat16)
        grad_down = jnp.einsum("sf,sd->fd", active, grad_low, preferred_element_type=jnp.float32)
        grad_active = jnp.einsum("sd,fd->sf", grad_low, w_down, preferred_element_type=jnp.float32)
        grad_lifted = gelu_back(grad_active)[0].astype(jnp.bfloat16)
        grad_up = jnp.einsum(
            "sd,sf->df", normed_two, grad_lifted, preferred_element_type=jnp.float32
        )
        grad_norm_two = lax.psum(
            jnp.einsum("sf,df->sd", grad_lifted, w_up, preferred_element_type=jnp.float32).astype(
                jnp.bfloat16
            ),
            "mp",
        ).astype(jnp.float32)
        grad_gain_two = jnp.sum(grad_norm_two * unit_two, axis=0)
        grad_shift_two = jnp.sum(grad_norm_two, axis=0)
        grad_resid = grad_out + norm_backward(grad_norm_two, unit_two, inverse_two, gain_two)
        grad_attn = grad_resid.astype(jnp.bfloat16)
        grad_wout = jnp.einsum(
            "sk,sd->kd", heads_out, grad_attn, preferred_element_type=jnp.float32
        )
        grad_heads = (
            jnp.einsum("sd,kd->sk", grad_attn, w_out, preferred_element_type=jnp.float32)
            .astype(jnp.bfloat16)
            .reshape(seq_len, heads_dev, HD)
        )
        grad_query, grad_key, grad_value = attend_backward(
            query_all, key_rows, value_rows, grad_heads, log_total, block_rows, score_scale
        )
        grad_pairs = jnp.stack(
            [grad_key.reshape(CTX, heads_dev * HD), grad_value.reshape(CTX, heads_dev * HD)]
        )
        grad_wqkv = jnp.concatenate(
            [
                jnp.einsum("sd,sn->dn", normed, grad_query, preferred_element_type=jnp.float32)[
                    :, None
                ],
                jnp.einsum("sd,csn->dcn", context, grad_pairs, preferred_element_type=jnp.float32),
            ],
            axis=1,
        )
        context_part = jnp.einsum(
            "csn,dcn->sd", grad_pairs, w_qkv[:, 1:], preferred_element_type=jnp.float32
        )
        grad_norm_part = jnp.einsum(
            "sn,dn->sd", grad_query, w_qkv[:, 0], preferred_element_type=jnp.float32
        )
        grad_norm_part = grad_norm_part + jnp.concatenate(
            [context_part, jnp.zeros((seq_len - CTX, width), jnp.float32)], axis=0
        )
        grad_norm_one = lax.psum(grad_norm_part.astype(jnp.bfloat16), "mp").astype(jnp.float32)
        grad_gain_one = jnp.sum(grad_norm_one * unit_one, axis=0)
        grad_shift_one = jnp.sum(grad_norm_one, axis=0)
        grad_list.append(grad_resid + norm_backward(grad_norm_one, unit_one, inverse_one, gain_one))
        table_grads = (
            grad_wqkv,
            grad_wout,
            grad_up,
            grad_down,
            grad_gain_one,
            grad_shift_one,
            grad_gain_two,
            grad_shift_two,
        )
        totals = table_grads if totals is None else jax.tree.map(jnp.add, totals, table_grads)
    totals = reduce_total(totals)
    return (
        jnp.stack(results),
        jnp.stack(grad_list),
        totals[0],
        totals[1],
        totals[2],
        totals[3],
        totals[4],
        totals[5],
        totals[6],
        totals[7],
    )


def solution(mesh):
    in_specs = (
        P("dp", None, None),
        P("dp"),
        P(None, None, "mp"),
        P("mp", None),
        P(None, "mp"),
        P("mp", None),
        P(),
        P(),
        P(),
        P(),
        P("dp", None, None),
    )
    out_specs = (
        P("dp", None, None),
        P("dp", None, None),
        P("dp", None, "mp"),
        P("mp", "dp"),
        P("dp", "mp"),
        P("mp", "dp"),
        P("dp"),
        P("dp"),
        P("dp"),
        P("dp"),
    )
    return jax.shard_map(
        per_device, mesh=mesh, in_specs=in_specs, out_specs=out_specs, check_vma=False
    )
```

profile of v0, /device:TPU:0, one launch (start us, length us, event | category | flops | bytes accessed | tf_op | source)
XLA Modules:
  0.0 761.9 jit_solution(2233834308572963741)
XLA Ops:
  19.3 22.0 %all-reduce.14.cloned.1.call-done = bf16[512,768]{1,0:T(8,128)(2,1)} async-done(((bf16[512,768]{1,0:T(8,128)(2,1)}), bf16[512,768]{1,0:T(8,128)(2,1)}) %all-reduce.14.cloned.1.call-update) | async-done | bytes 786448 | tf_op jit(solution)/shard_map/psum | solution.py:143
  41.3 2.2 fusion.81
  57.0 18.3 %all-reduce.16.cloned.1.call-done = bf16[512,768]{1,0:T(8,128)(2,1)} async-done(((bf16[512,768]{1,0:T(8,128)(2,1)}), bf16[512,768]{1,0:T(8,128)(2,1)}) %all-reduce.16.cloned.1.call-update) | async-done | bytes 786448 | tf_op jit(solution)/shard_map/psum | solution.py:143
  75.3 2.6 multiply_reduce_fusion.5
  78.6 8.9 %multiply_convert_fusion.2 = (bf16[512,1536]{1,0:T(8,128)(2,1)}, f32[512,1536]{1,0:T(8,128)S(1)}, f32[512,1536]{1,0:T(8,128)S(1)}) fusion(bf16[768,1536]{1,0:T(8,128)(2,1)S(1)} %copy-done, f32[768]{0:T(1024)S(1)} %copy-done.56, f32[768]{0:T(1024)S(1)} %copy-done.55, f32[512]{0:T(512)S(1)} %add_rsqrt_fusion, f32[512]{0:T(512)S(1)} %get-tuple-element.163, ...), kind=kOutput, calls=%fused_computation.24 | convolution fusion | flops 1262223360 | bytes 11808768 | tf_op jit(solution)/shard_map/dot_general | solution.py:149
  87.5 2.2 add_convert_fusion
  89.7 2.3 convolution_convert_fusion
  92.1 21.4 %multiply_convert_fusion.3 = (bf16[512,1536]{1,0:T(8,128)(2,1)}, f32[512,1536]{1,0:T(8,128)S(1)}, f32[512,1536]{1,0:T(8,128)S(1)}) fusion(bf16[768,1536]{1,0:T(8,128)(2,1)S(1)} %copy-done, f32[768]{0:T(1024)S(1)} %copy-done.56, f32[768]{0:T(1024)S(1)} %copy-done.55, f32[512]{0:T(512)S(1)} %get-tuple-element.162, f32[512]{0:T(512)S(1)} %broadcast_multiply_fusion.10, ...), kind=kOutput, calls=%fused_computation.37 | convolution fusion | flops 1262223360 | bytes 11808768 | tf_op jit(solution)/shard_map/dot_general | solution.py:149
  113.5 2.2 add_convert_fusion.1
  116.8 2.3 convolution_convert_fusion.1
  120.6 4.1 convolution_convert_fusion.2
  124.7 2.3 convolution_convert_fusion.3
  127.0 14.0 %all-reduce.20.cloned.1.call-done = (bf16[512,768]{1,0:T(8,128)(2,1)}, bf16[512,768]{1,0:T(8,128)(2,1)}) async-done(((bf16[512,768]{1,0:T(8,128)(2,1)}, bf16[512,768]{1,0:T(8,128)(2,1)}), (bf16[512,768]{1,0:T(8,128)(2,1)}, bf16[512,768]{1,0:T(8,128)(2,1)})) %all-reduce.20.cloned.1.call-update) | async-done | bytes 1572880 | tf_op jit(solution)/shard_map/psum | solution.py:164
  141.0 3.7 fusion.74
  144.8 3.1 fusion.64
  165.2 2.0 copy.51
  169.0 1.9 copy.44
  170.8 2.3 convolution_bitcast_fusion
  178.2 2.2 fusion.116
  188.4 2.2 maximum_add_fusion
  191.3 3.2 fusion.136
  194.5 4.2 convolution_add_fusion.1
  199.3 3.4 fusion.125
  202.7 3.8 convolution_add_fusion
  208.6 3.8 fusion.75
  212.4 77.1 %all-reduce.6 = (f32[768]{0:T(1024)S(1)}, f32[768]{0:T(1024)S(1)}, f32[768]{0:T(1024)S(1)}, f32[768]{0:T(1024)S(1)}) all-reduce(f32[768]{0:T(1024)S(1)} %add.239, f32[768]{0:T(1024)S(1)} %add.240, f32[768]{0:T(1024)S(1)} %add.241, f32[768]{0:T(1024)S(1)} %add.242), channel_id=6, replica_groups=mesh['dp'=16,'mp'=2] {'dp'}, use_global_device_ids=true, to_apply=%region_36.37.clone | all-reduce | flops 3072 | bytes 24576
  291.9 3.4 fusion.60
  296.6 1.9 pad_maximum_fusion
  298.5 33.4 %reduce-scatter.7.cloned.1.call-done = f32[384,48]{0,1:T(8,128)} async-done(((f32[384,768]{0,1:T(8,128)}), f32[384,48]{0,1:T(8,128)}) %reduce-scatter.7.cloned.1.call-update) | async-done | bytes 73744 | tf_op jit(solution)/shard_map/reduce_scatter | solution.py:103
  331.9 138.1 %reduce-scatter.5.cloned.1.call-done = f32[48,3,384]{2,0,1:T(8,128)} async-done(((f32[768,3,384]{2,0,1:T(8,128)}), f32[48,3,384]{2,0,1:T(8,128)}) %reduce-scatter.5.cloned.1.call-update) | async-done | bytes 221200 | tf_op jit(solution)/shard_map/reduce_scatter | solution.py:102
  469.9 142.4 %reduce-scatter.9.cloned.1.call-done = f32[48,1536]{1,0:T(8,128)} async-done(((f32[768,1536]{1,0:T(8,128)}), f32[48,1536]{1,0:T(8,128)}) %reduce-scatter.9.cloned.1.call-update) | async-done | bytes 294928 | tf_op jit(solution)/shard_map/reduce_scatter | solution.py:104
  612.3 142.3 %reduce-scatter.11.cloned.1.call-done = f32[1536,48]{0,1:T(8,128)} async-done(((f32[1536,768]{0,1:T(8,128)}), f32[1536,48]{0,1:T(8,128)}) %reduce-scatter.11.cloned.1.call-update) | async-done | bytes 294928 | tf_op jit(solution)/shard_map/reduce_scatter | solution.py:105
  (277 shorter events, 65.0 us)
Async XLA Ops:
  7.2 71.2 %copy-start = (bf16[768,1536]{1,0:T(8,128)(2,1)S(1)}, bf16[768,1536]{1,0:T(8,128)(2,1)}, u32[]{:S(2)}) copy-start(bf16[768,1536]{1,0:T(8,128)(2,1)} %param.15) | copy-start | bytes 7077892
  7.2 34.1 %all-reduce.14.cloned.1.call-start = ((), (), s32[]{:S(2)}) async-start(), calls=%async_computation.4 | async-start | bytes 1572864 | tf_op jit(solution)/shard_map/psum | solution.py:143
  19.2 56.0 %all-reduce.16.cloned.1.call-start = ((), (), s32[]{:S(2)}) async-start(), calls=%async_computation.5 | async-start | bytes 1572864 | tf_op jit(solution)/shard_map/psum | solution.py:143
  19.3 26.0 %copy-start.61 = (f32[512]{0:T(512)}, f32[512]{0:T(512)S(1)}, u32[]{:S(2)}) copy-start(f32[512]{0:T(512)S(1)} %broadcast_multiply_fusion.9) | copy-start | bytes 6148
  54.7 86.3 %all-reduce.20.cloned.1.call-start = ((), (), s32[]{:S(2)}) async-start(), calls=%async_computation.11 | async-start | bytes 3145728 | tf_op jit(solution)/shard_map/psum | solution.py:164
  56.9 87.8 %copy-start.70 = (f32[512]{0:T(512)}, f32[512]{0:T(512)S(1)}, u32[]{:S(2)}) copy-start(f32[512]{0:T(512)S(1)} %get-tuple-element.164) | copy-start | bytes 6148
  56.9 87.8 %copy-start.72 = (f32[512]{0:T(512)}, f32[512]{0:T(512)S(1)}, u32[]{:S(2)}) copy-start(f32[512]{0:T(512)S(1)} %get-tuple-element.165) | copy-start | bytes 6148
  56.9 87.8 %copy-start.74 = (f32[512]{0:T(512)}, f32[512]{0:T(512)S(1)}, u32[]{:S(2)}) copy-start(f32[512]{0:T(512)S(1)} %broadcast_multiply_fusion.10) | copy-start | bytes 6148
  77.9 14.2 %copy-start.76 = (f32[512]{0:T(512)}, f32[512]{0:T(512)S(1)}, u32[]{:S(2)}) copy-start(f32[512]{0:T(512)S(1)} %get-tuple-element.162) | copy-start | bytes 6148
  78.6 66.2 %copy-start.63 = (f32[512]{0:T(512)}, f32[512]{0:T(512)S(1)}, u32[]{:S(2)}) copy-start(f32[512]{0:T(512)S(1)} %add_rsqrt_fusion) | copy-start | bytes 6148
  78.6 8.9 %copy-start.16 = (bf16[2,512,768]{2,1,0:T(8,128)(2,1)S(1)}, bf16[2,512,768]{2,1,0:T(8,128)(2,1)}, u32[]{:S(2)}) copy-start(bf16[2,512,768]{2,1,0:T(8,128)(2,1)} %param.21) | copy-start | bytes 4718596
  78.6 8.9 %copy-start.86 = (bf16[1536,768]{1,0:T(8,128)(2,1)S(1)}, bf16[1536,768]{1,0:T(8,128)(2,1)}, u32[]{:S(2)}) copy-start(bf16[1536,768]{1,0:T(8,128)(2,1)} %param.16) | copy-start | bytes 7077892
  119.2 89.4 %all-reduce.18.cloned.1.call-start = ((), (), s32[]{:S(2)}) async-start(), calls=%async_computation.10 | async-start | bytes 6291456 | tf_op jit(solution)/shard_map/psum | solution.py:152
  120.6 4.1 copy-start.27
  120.6 4.1 copy-start.87
  124.6 16.4 %copy-start.5 = (bf16[2,512,768]{2,1,0:T(8,128)(2,1)S(1)}, bf16[2,512,768]{2,1,0:T(8,128)(2,1)}, u32[]{:S(2)}) copy-start(bf16[2,512,768]{2,1,0:T(8,128)(2,1)} %param.11) | copy-start | bytes 4718596
  124.6 16.4 %copy-start.13 = (bf16[512,768]{1,0:T(8,128)(2,1)S(1)}, bf16[512,768]{1,0:T(8,128)(2,1)}, u32[]{:S(2)}) copy-start(bf16[512,768]{1,0:T(8,128)(2,1)} %all-reduce.14.cloned.1.call-done) | copy-start | bytes 2359300
  124.6 16.4 %copy-start.77 = (f32[512]{0:T(512)S(1)}, f32[512]{0:T(512)}, u32[]{:S(2)}) copy-start(f32[512]{0:T(512)} %copy-done.76) | copy-start | bytes 6148
  141.0 8.1 %slice-start.2 = ((s8[4718592]{0:T(1024)(128)(4,1)}), s8[4194304]{0:T(1024)(128)(4,1)S(1)}, s32[]{:S(2)}) async-start(s8[4718592]{0:T(1024)(128)(4,1)} %bitcast.232), calls=%async_computation.14 | async-start | bytes 8388608
  144.8 4.3 slice-start.3
  147.9 8.4 %copy-start.9 = (f32[512,768]{1,0:T(8,128)}, f32[512,768]{1,0:T(8,128)S(1)}, u32[]{:S(2)}) copy-start(f32[512,768]{1,0:T(8,128)S(1)} %get-tuple-element.140) | copy-start | bytes 4718596
  150.8 6.1 slice-start
  152.0 4.8 slice-start.1
  165.2 9.6 %copy-start.42 = (bf16[1,384,384]{2,1,0:T(8,128)(2,1)}, bf16[1,384,384]{2,1,0:T(8,128)(2,1)S(1)}, u32[]{:S(2)}) copy-start(bf16[1,384,384]{2,1,0:T(8,128)(2,1)S(1)} %copy.45) | copy-start | bytes 884740
  177.2 154.6 %reduce-scatter.7.cloned.1.call-start = ((), (), s32[]{:S(2)}) async-start(), calls=%async_computation.7 | async-start | bytes 1253376 | tf_op jit(solution)/shard_map/reduce_scatter | solution.py:103
  182.1 287.8 %reduce-scatter.5.cloned.1.call-start = ((), (), s32[]{:S(2)}) async-start(), calls=%async_computation.6 | async-start | bytes 3760128 | tf_op jit(solution)/shard_map/reduce_scatter | solution.py:102
  190.7 3.8 copy-start.64
  190.7 421.7 %reduce-scatter.9.cloned.1.call-start = ((), (), s32[]{:S(2)}) async-start(), calls=%async_computation.8 | async-start | bytes 5013504 | tf_op jit(solution)/shard_map/reduce_scatter | solution.py:104
  198.7 4.0 copy-start.73
  198.7 555.9 %reduce-scatter.11.cloned.1.call-start = ((), (), s32[]{:S(2)}) async-start(), calls=%async_computation.9 | async-start | bytes 5013504 | tf_op jit(solution)/shard_map/reduce_scatter | solution.py:105
  291.8 3.4 copy-start.24
  296.6 458.0 %copy-start.1 = (bf16[768,1536]{1,0:T(8,128)(2,1)S(1)}, bf16[768,1536]{1,0:T(8,128)(2,1)}, u32[]{:S(2)}) copy-start(bf16[768,1536]{1,0:T(8,128)(2,1)} %param.15) | copy-start | bytes 7077892
  (70 other events, 119.6 us)
Sparse Core Ops, SparseCore 0:
  19.3 21.8 all-reduce.13
  54.8 20.3 all-reduce.15
  119.3 21.6 all-reduce.19
  177.4 24.5 all-reduce.17
  207.1 124.6 reduce-scatter.6
  337.4 132.4 reduce-scatter.4
  475.7 136.6 reduce-scatter.8
  618.9 135.6 reduce-scatter.10
where the time goes:
time: 771 us; the launch traced here: 762 us
  waiting for transfers between devices  511 us (66%)
  matrix products  97.8 us (13%)
  blocking collectives  77.1 us (10%)
  other arithmetic  31.8 us (4%)
  local copies, waits for them, and re-layouts  26.1 us (3%)
  between operations  17.6 us (2%)
    reduce_scatter x1, waiting for transfers between devices, reduce_total(): lax.psum_scatter(grads[2], 'dp', scatter_dimension=0, tiled=True)  142 us
    reduce_scatter x1, waiting for transfers between devices, reduce_total(): lax.psum_scatter(grads[3], 'dp', scatter_dimension=1, tiled=True)  142 us
    reduce_scatter x1, waiting for transfers between devices, reduce_total(): lax.psum_scatter(grads[0], 'dp', scatter_dimension=0, tiled=True)  138 us
    unnamed x1, blocking collectives  77.1 us
    psum x2, waiting for transfers between devices, per_device(): lax.psum(jnp.dot(heads_out, w_out, preferred_element_type=jnp.float32).as...  40.3 us
    reduce_scatter x1, waiting for transfers between devices, reduce_total(): lax.psum_scatter(grads[1], 'dp', scatter_dimension=1, tiled=True)  33.4 us
    dot_general x2, matrix products, per_device(): lifted = jnp.dot(normed_two, w_up, preferred_element_type=jnp.float32)  30.3 us
    unnamed x193, local copies, waits for them, and re-layouts  18.6 us
  transfers between devices with their start and end apart: 8, of which 7 were waited for; matrix products, arithmetic and copies ran while one was open for 6% of the time, Pallas kernels for 0%

commit v1 on v0

--- a/solution.py
+++ b/solution.py
@@ -140,8 +140,12 @@
         heads_out, log_total = attend_forward(
             query_all, key_rows, value_rows, block_rows, score_scale
         )
-        attended = lax.psum(
-            jnp.dot(heads_out, w_out, preferred_element_type=jnp.float32).astype(jnp.bfloat16), "mp"
+        attended = jnp.sum(
+            lax.all_gather(
+                jnp.dot(heads_out, w_out, preferred_element_type=jnp.float32).astype(jnp.bfloat16),
+                "mp",
+            ),
+            axis=0,
         ).astype(jnp.float32)
         resid = row_data + attended
         unit_two, inverse_two, normed_two = layer_norm(resid, gain_two, shift_two)

time: 771 us -> 744 us (0.965)
  waiting for transfers between devices: 511 us -> 491 us
  matrix products: 97.8 us -> 85.6 us
    psum x2 -> x0, waiting for transfers between devices: 40.3 us -> none  [per_device(): lax.psum(jnp.dot(heads_out, w_out, preferred_element_type=jnp.float32).as...]
    all_gather x0 -> x2, waiting for transfers between devices: none -> 21.5 us  [per_device(): lax.all_gather(jnp.dot(heads_out, w_out, preferred_element_type=jnp.float...]
    dot_general x2, matrix products: 30.3 us -> 18.2 us  [per_device(): lifted = jnp.dot(normed_two, w_up, preferred_element_type=jnp.float32)]
    unnamed x193 -> x195, local copies, waits for them, and re-layouts: 18.6 us -> 18.6 us
where the time goes in v1:
time: 744 us; the launch traced here: 735 us
  waiting for transfers between devices  491 us (66%)
  matrix products  85.6 us (12%)
  blocking collectives  77.2 us (10%)
  other arithmetic  35.8 us (5%)
  local copies, waits for them, and re-layouts  26.2 us (4%)
  between operations  17.7 us (2%)
    reduce_scatter x1, waiting for transfers between devices, reduce_total(): lax.psum_scatter(grads[3], 'dp', scatter_dimension=1, tiled=True)  143 us
    reduce_scatter x1, waiting for transfers between devices, reduce_total(): lax.psum_scatter(grads[2], 'dp', scatter_dimension=0, tiled=True)  141 us
    reduce_scatter x1, waiting for transfers between devices, reduce_total(): lax.psum_scatter(grads[0], 'dp', scatter_dimension=0, tiled=True)  138 us
    unnamed x1, blocking collectives  77.2 us
    reduce_scatter x1, waiting for transfers between devices, reduce_total(): lax.psum_scatter(grads[1], 'dp', scatter_dimension=1, tiled=True)  33.4 us
    all_gather x2, waiting for transfers between devices, per_device(): lax.all_gather(jnp.dot(heads_out, w_out, preferred_element_type=jnp.float...  21.5 us
    unnamed x195, local copies, waits for them, and re-layouts  18.6 us
    dot_general x2, matrix products, per_device(): lifted = jnp.dot(normed_two, w_up, preferred_element_type=jnp.float32)  18.2 us
  transfers between devices with their start and end apart: 8, of which 7 were waited for; matrix products, arithmetic and copies ran while one was open for 6% of the time, Pallas kernels for 0%

profile of v1, /device:TPU:0, one launch (start us, length us, event | category | flops | bytes accessed | tf_op | source)
XLA Modules:
  0.0 734.7 jit_solution(8688780927319872694)
XLA Ops:
  19.3 12.6 %all-gather.5.cloned.1.call-done = bf16[1024,768]{1,0:T(8,128)(2,1)} async-done(((bf16[512,768]{1,0:T(8,128)(2,1)}), bf16[1024,768]{1,0:T(8,128)(2,1)}) %all-gather.5.cloned.1.call-update) | async-done | bytes 1572880 | tf_op jit(solution)/shard_map/all_gather | solution.py:144
  31.9 2.1 reduce_sum.283
  34.0 2.2 fusion.81
  49.6 8.9 %all-gather.7.cloned.1.call-done = bf16[1024,768]{1,0:T(8,128)(2,1)} async-done(((bf16[512,768]{1,0:T(8,128)(2,1)}), bf16[1024,768]{1,0:T(8,128)(2,1)}) %all-gather.7.cloned.1.call-update) | async-done | bytes 1572880 | tf_op jit(solution)/shard_map/all_gather | solution.py:144
  58.5 2.1 reduce_sum.289
  60.7 2.3 multiply_reduce_fusion.5
  63.7 8.9 %multiply_convert_fusion.2 = (bf16[512,1536]{1,0:T(8,128)(2,1)}, f32[512,1536]{1,0:T(8,128)S(1)}, f32[512,1536]{1,0:T(8,128)S(1)}) fusion(bf16[768,1536]{1,0:T(8,128)(2,1)S(1)} %copy-done, f32[768]{0:T(1024)S(1)} %copy-done.57, f32[768]{0:T(1024)S(1)} %copy-done.56, f32[512]{0:T(512)S(1)} %add_rsqrt_fusion, f32[512]{0:T(512)S(1)} %get-tuple-element.163, ...), kind=kOutput, calls=%fused_computation.24 | convolution fusion | flops 1262223360 | bytes 11808768 | tf_op jit(solution)/shard_map/dot_general | solution.py:153
  72.6 2.2 add_convert_fusion
  74.9 2.3 convolution_convert_fusion
  77.2 9.3 %multiply_convert_fusion.3 = (bf16[512,1536]{1,0:T(8,128)(2,1)}, f32[512,1536]{1,0:T(8,128)S(1)}, f32[512,1536]{1,0:T(8,128)S(1)}) fusion(bf16[768,1536]{1,0:T(8,128)(2,1)S(1)} %copy-done, f32[768]{0:T(1024)S(1)} %copy-done.57, f32[768]{0:T(1024)S(1)} %copy-done.56, f32[512]{0:T(512)S(1)} %get-tuple-element.162, f32[512]{0:T(512)S(1)} %broadcast_multiply_fusion.10, ...), kind=kOutput, calls=%fused_computation.37 | convolution fusion | flops 1262223360 | bytes 11808768 | tf_op jit(solution)/shard_map/dot_general | solution.py:153
  86.5 2.2 add_convert_fusion.1
  89.8 2.3 convolution_convert_fusion.1
  93.6 4.1 convolution_convert_fusion.2
  97.7 2.3 convolution_convert_fusion.3
  100.0 14.0 %all-reduce.14.cloned.1.call-done = (bf16[512,768]{1,0:T(8,128)(2,1)}, bf16[512,768]{1,0:T(8,128)(2,1)}) async-done(((bf16[512,768]{1,0:T(8,128)(2,1)}, bf16[512,768]{1,0:T(8,128)(2,1)}), (bf16[512,768]{1,0:T(8,128)(2,1)}, bf16[512,768]{1,0:T(8,128)(2,1)})) %all-reduce.14.cloned.1.call-update) | async-done | bytes 1572880 | tf_op jit(solution)/shard_map/psum | solution.py:168
  114.0 3.7 fusion.74
  117.8 3.3 fusion.64
  138.4 2.0 copy.51
  144.0 2.3 convolution_bitcast_fusion
  151.4 2.2 fusion.116
  161.6 2.2 maximum_add_fusion
  164.5 3.2 fusion.136
  167.7 4.2 convolution_add_fusion.1
  172.5 3.4 fusion.125
  175.9 3.8 convolution_add_fusion
  181.8 3.8 fusion.75
  185.6 77.2 %all-reduce.6 = (f32[768]{0:T(1024)S(1)}, f32[768]{0:T(1024)S(1)}, f32[768]{0:T(1024)S(1)}, f32[768]{0:T(1024)S(1)}) all-reduce(f32[768]{0:T(1024)S(1)} %add.235, f32[768]{0:T(1024)S(1)} %add.236, f32[768]{0:T(1024)S(1)} %add.237, f32[768]{0:T(1024)S(1)} %add.238), channel_id=8, replica_groups=mesh['dp'=16,'mp'=2] {'dp'}, use_global_device_ids=true, to_apply=%region_36.37.clone | all-reduce | flops 3072 | bytes 24576
  265.1 3.4 fusion.60
  271.7 33.4 %reduce-scatter.7.cloned.1.call-done = f32[384,48]{0,1:T(8,128)} async-done(((f32[384,768]{0,1:T(8,128)}), f32[384,48]{0,1:T(8,128)}) %reduce-scatter.7.cloned.1.call-update) | async-done | bytes 73744 | tf_op jit(solution)/shard_map/reduce_scatter | solution.py:103
  305.1 138.3 %reduce-scatter.5.cloned.1.call-done = f32[48,3,384]{2,0,1:T(8,128)} async-done(((f32[768,3,384]{2,0,1:T(8,128)}), f32[48,3,384]{2,0,1:T(8,128)}) %reduce-scatter.5.cloned.1.call-update) | async-done | bytes 221200 | tf_op jit(solution)/shard_map/reduce_scatter | solution.py:102
  443.4 141.5 %reduce-scatter.9.cloned.1.call-done = f32[48,1536]{1,0:T(8,128)} async-done(((f32[768,1536]{1,0:T(8,128)}), f32[48,1536]{1,0:T(8,128)}) %reduce-scatter.9.cloned.1.call-update) | async-done | bytes 294928 | tf_op jit(solution)/shard_map/reduce_scatter | solution.py:104
  584.8 142.7 %reduce-scatter.11.cloned.1.call-done = f32[1536,48]{0,1:T(8,128)} async-done(((f32[1536,768]{0,1:T(8,128)}), f32[1536,48]{0,1:T(8,128)}) %reduce-scatter.11.cloned.1.call-update) | async-done | bytes 294928 | tf_op jit(solution)/shard_map/reduce_scatter | solution.py:105
  (282 shorter events, 68.8 us)
Async XLA Ops:
  7.2 56.3 %copy-start = (bf16[768,1536]{1,0:T(8,128)(2,1)S(1)}, bf16[768,1536]{1,0:T(8,128)(2,1)}, u32[]{:S(2)}) copy-start(bf16[768,1536]{1,0:T(8,128)(2,1)} %param.15) | copy-start | bytes 7077892
  7.2 24.7 %all-gather.5.cloned.1.call-start = ((), (), s32[]{:S(2)}) async-start(), calls=%async_computation.8 | async-start | bytes 2359296 | tf_op jit(solution)/shard_map/all_gather | solution.py:144
  19.2 39.3 %all-gather.7.cloned.1.call-start = ((), (), s32[]{:S(2)}) async-start(), calls=%async_computation.9 | async-start | bytes 2359296 | tf_op jit(solution)/shard_map/all_gather | solution.py:144
  19.3 18.7 %copy-start.62 = (f32[512]{0:T(512)}, f32[512]{0:T(512)S(1)}, u32[]{:S(2)}) copy-start(f32[512]{0:T(512)S(1)} %broadcast_multiply_fusion.9) | copy-start | bytes 6148
  34.0 4.0 copy-start.8
  47.4 66.6 %all-reduce.14.cloned.1.call-start = ((), (), s32[]{:S(2)}) async-start(), calls=%async_computation.11 | async-start | bytes 3145728 | tf_op jit(solution)/shard_map/psum | solution.py:168
  49.6 68.2 %copy-start.71 = (f32[512]{0:T(512)}, f32[512]{0:T(512)S(1)}, u32[]{:S(2)}) copy-start(f32[512]{0:T(512)S(1)} %fusion.143) | copy-start | bytes 6148
  49.6 68.1 %copy-start.73 = (f32[512]{0:T(512)}, f32[512]{0:T(512)S(1)}, u32[]{:S(2)}) copy-start(f32[512]{0:T(512)S(1)} %fusion.144) | copy-start | bytes 6148
  49.6 68.1 %copy-start.75 = (f32[512]{0:T(512)}, f32[512]{0:T(512)S(1)}, u32[]{:S(2)}) copy-start(f32[512]{0:T(512)S(1)} %broadcast_multiply_fusion.10) | copy-start | bytes 6148
  63.0 14.1 %copy-start.77 = (f32[512]{0:T(512)}, f32[512]{0:T(512)S(1)}, u32[]{:S(2)}) copy-start(f32[512]{0:T(512)S(1)} %get-tuple-element.162) | copy-start | bytes 6148
  63.7 54.1 %copy-start.64 = (f32[512]{0:T(512)}, f32[512]{0:T(512)S(1)}, u32[]{:S(2)}) copy-start(f32[512]{0:T(512)S(1)} %add_rsqrt_fusion) | copy-start | bytes 6148
  63.7 8.9 %copy-start.17 = (bf16[2,512,768]{2,1,0:T(8,128)(2,1)S(1)}, bf16[2,512,768]{2,1,0:T(8,128)(2,1)}, u32[]{:S(2)}) copy-start(bf16[2,512,768]{2,1,0:T(8,128)(2,1)} %param.21) | copy-start | bytes 4718596
  63.7 8.9 %copy-start.87 = (bf16[1536,768]{1,0:T(8,128)(2,1)S(1)}, bf16[1536,768]{1,0:T(8,128)(2,1)}, u32[]{:S(2)}) copy-start(bf16[1536,768]{1,0:T(8,128)(2,1)} %param.16) | copy-start | bytes 7077892
  92.2 89.6 %all-reduce.12.cloned.1.call-start = ((), (), s32[]{:S(2)}) async-start(), calls=%async_computation.10 | async-start | bytes 6291456 | tf_op jit(solution)/shard_map/psum | solution.py:156
  93.6 4.1 copy-start.28
  93.6 4.1 copy-start.88
  97.6 16.3 %copy-start.5 = (bf16[2,512,768]{2,1,0:T(8,128)(2,1)S(1)}, bf16[2,512,768]{2,1,0:T(8,128)(2,1)}, u32[]{:S(2)}) copy-start(bf16[2,512,768]{2,1,0:T(8,128)(2,1)} %param.11) | copy-start | bytes 4718596
  97.6 16.3 %copy-start.10 = (bf16[512,768]{1,0:T(8,128)(2,1)S(1)}, bf16[512,768]{1,0:T(8,128)(2,1)}, u32[]{:S(2)}) copy-start(bf16[512,768]{1,0:T(8,128)(2,1)} %copy-done.8) | copy-start | bytes 2359300
  97.7 16.3 %copy-start.78 = (f32[512]{0:T(512)S(1)}, f32[512]{0:T(512)}, u32[]{:S(2)}) copy-start(f32[512]{0:T(512)} %copy-done.77) | copy-start | bytes 6148
  114.0 8.3 %slice-start.2 = ((s8[4718592]{0:T(1024)(128)(4,1)}), s8[4194304]{0:T(1024)(128)(4,1)S(1)}, s32[]{:S(2)}) async-start(s8[4718592]{0:T(1024)(128)(4,1)} %bitcast.234), calls=%async_computation.14 | async-start | bytes 8388608
  117.8 4.5 slice-start.3
  121.1 8.4 %copy-start.11 = (f32[512,768]{1,0:T(8,128)}, f32[512,768]{1,0:T(8,128)S(1)}, u32[]{:S(2)}) copy-start(f32[512,768]{1,0:T(8,128)S(1)} %get-tuple-element.140) | copy-start | bytes 4718596
  124.0 6.1 slice-start
  125.2 4.8 slice-start.1
  138.3 9.6 %copy-start.43 = (bf16[1,384,384]{2,1,0:T(8,128)(2,1)}, bf16[1,384,384]{2,1,0:T(8,128)(2,1)S(1)}, u32[]{:S(2)}) copy-start(bf16[1,384,384]{2,1,0:T(8,128)(2,1)S(1)} %copy.45) | copy-start | bytes 884740
  150.4 154.7 %reduce-scatter.7.cloned.1.call-start = ((), (), s32[]{:S(2)}) async-start(), calls=%async_computation.5 | async-start | bytes 1253376 | tf_op jit(solution)/shard_map/reduce_scatter | solution.py:103
  155.3 288.1 %reduce-scatter.5.cloned.1.call-start = ((), (), s32[]{:S(2)}) async-start(), calls=%async_computation.4 | async-start | bytes 3760128 | tf_op jit(solution)/shard_map/reduce_scatter | solution.py:102
  163.9 3.8 copy-start.65
  163.9 421.0 %reduce-scatter.9.cloned.1.call-start = ((), (), s32[]{:S(2)}) async-start(), calls=%async_computation.6 | async-start | bytes 5013504 | tf_op jit(solution)/shard_map/reduce_scatter | solution.py:104
  171.9 4.0 copy-start.74
  171.9 555.6 %reduce-scatter.11.cloned.1.call-start = ((), (), s32[]{:S(2)}) async-start(), calls=%async_computation.7 | async-start | bytes 5013504 | tf_op jit(solution)/shard_map/reduce_scatter | solution.py:105
  269.8 457.7 %copy-start.1 = (bf16[768,1536]{1,0:T(8,128)(2,1)S(1)}, bf16[768,1536]{1,0:T(8,128)(2,1)}, u32[]{:S(2)}) copy-start(bf16[768,1536]{1,0:T(8,128)(2,1)} %param.15) | copy-start | bytes 7077892
  (71 other events, 122.2 us)
Sparse Core Ops, SparseCore 0:
  19.3 12.4 all-gather.4
  47.5 10.9 all-gather.6
  92.3 21.6 all-reduce.13
  150.5 24.5 all-reduce.11
  180.3 124.7 reduce-scatter.6
  310.6 132.6 reduce-scatter.4
  449.1 135.6 reduce-scatter.8
  591.4 136.0 reduce-scatter.10
